TPU v7x, 32 devices: a whole 2x2x4 slice. The times are simulated.
32 devices in a mesh: outer: 4 (over y, x), inner: 8 (over z, core).
Axes of the slice: x: 2, y: 2, z: 4, core: 2. Of those that a mesh axis runs over, the one named last changes fastest.
Arguments:
- inputs: bfloat16 [8192, 8192], P(('outer', 'inner')), may hold values from -6 to 6
- step_size: float32 [8192, 128], P(('outer', 'inner')), may hold values from 0 to 1
- log_decay: float32 [8192, 128], P(('outer', 'inner')), may hold values from -1.25 to 0
- b_matrix: bfloat16 [8192, 1024], P(('outer', 'inner')), may hold values from -1 to 1
- c_matrix: bfloat16 [8192, 1024], P(('outer', 'inner')), may hold values from -1 to 1
- skip_gain: float32 [128], replicated, may hold values from 0.5 to 1.5
Outputs:
- mixed: bfloat16 [8192, 8192], P(('outer', 'inner'))
All inputs are finite; a program needn't handle non-finite values.
Results may differ from a plain program's by a relative error of at most 0.006.
Values may be sent and summed in bfloat16 or wider, within the bound.
No kernel may reach another device: no remote copies, remote signals or barrier semaphores. Data moves between devices by JAX's collectives and lax.ppermute only.
A program may use at most 128 MiB of HBM per device.

v0:
```python
import jax
import jax.numpy as jnp
from jax import lax
from jax.sharding import PartitionSpec as P

GROUPS = 8
BLOCK_LENGTH = 256
MIXED_PREC = lax.Precision.HIGH


def passed_along(block, axis, distance):
    devices = range(lax.axis_size(axis))
    route = [(i - distance, i) for i in devices if i - distance in devices]
    return lax.ppermute(block, axis, route)


def group_pass(scaled, decay_log, b_rows, c_rows):
    seq_rows, head_count, head_width = scaled.shape
    state_width = b_rows.shape[1]
    block_rows = min(BLOCK_LENGTH, seq_rows)
    per_turn = min(8, seq_rows // block_rows)
    turn_count = seq_rows // (block_rows * per_turn)
    lower_mask = jnp.tril(jnp.ones((block_rows, block_rows), dtype=bool))

    def advance(carried_pair, pieces):
        carried, offset = carried_pair
        scaled_part, log_part, b_part, c_part = pieces
        running = jnp.cumsum(log_part, axis=1)
        scores = jnp.einsum("ktn,ksn->kts", c_part, b_part, preferred_element_type=jnp.float32)
        spread = running[:, :, None, :] - running[:, None, :, :]
        weights = scores[..., None] * jnp.exp(
            jnp.where(lower_mask[None, :, :, None], spread, -jnp.inf)
        )
        as_float = scaled_part.astype(jnp.float32)
        within = jnp.einsum("ktsh,kshp->kthp", weights, as_float, precision=MIXED_PREC)
        span_total = running[:, -1, :]
        to_end = jnp.exp(span_total[:, None, :] - running)
        local_states = jnp.einsum(
            "kshp,ksn->khpn",
            as_float * to_end[..., None],
            b_part.astype(jnp.float32),
            precision=MIXED_PREC,
        )
        entering = []
        for member in range(per_turn):
            entering.append(carried)
            carried = jnp.exp(span_total[member])[:, None, None] * carried + local_states[member]
        entering = jnp.stack(entering)
        from_carry = (
            jnp.einsum("ktn,khpn->kthp", c_part.astype(jnp.float32), entering, precision=MIXED_PREC)
            * jnp.exp(running)[..., None]
        )
        before = jnp.cumsum(span_total, axis=0) - span_total + offset[None, :]
        return (
            (carried, offset + jnp.sum(span_total, axis=0)),
            (within + from_carry, running + before[:, None, :]),
        )

    start_pair = (
        jnp.zeros((head_count, head_width, state_width), jnp.float32),
        jnp.zeros((head_count,), jnp.float32),
    )
    pieces = (
        scaled.reshape(turn_count, per_turn, block_rows, head_count, head_width),
        decay_log.reshape(turn_count, per_turn, block_rows, head_count),
        b_rows.reshape(turn_count, per_turn, block_rows, state_width),
        c_rows.reshape(turn_count, per_turn, block_rows, state_width),
    )
    (end_state, block_log), (outputs, running_all) = lax.scan(advance, start_pair, pieces)
    return (
        outputs.reshape(seq_rows, head_count, head_width),
        end_state,
        block_log,
        running_all.reshape(seq_rows, head_count),
    )


def carry_chain(block_log, end_state):
    incoming = jnp.zeros_like(end_state)
    for handoff_turn in range(lax.axis_size("outer") - 1):
        incoming = passed_along(
            jnp.exp(block_log)[:, None, None] * incoming + end_state, "outer", 1
        )
    return incoming


def local(inputs, step_size, log_decay, b_matrix, c_matrix, skip_gain):
    tokens = inputs.shape[0]
    head_count = step_size.shape[1]
    head_width = inputs.shape[1] // head_count
    state_width = b_matrix.shape[1] // GROUPS
    inner_count = lax.axis_size("inner")
    heads_dev = head_count // inner_count
    copies = inner_count // GROUPS
    b_copy = jnp.repeat(b_matrix.reshape(tokens, GROUPS, state_width), copies, axis=1).reshape(
        tokens, inner_count * state_width
    )
    c_copy = jnp.repeat(c_matrix.reshape(tokens, GROUPS, state_width), copies, axis=1).reshape(
        tokens, inner_count * state_width
    )
    head_inputs, b_rows, c_rows = (
        lax.all_to_all(inputs, "inner", split_axis=1, concat_axis=0, tiled=True),
        lax.all_to_all(b_copy, "inner", split_axis=1, concat_axis=0, tiled=True),
        lax.all_to_all(c_copy, "inner", split_axis=1, concat_axis=0, tiled=True),
    )
    step_rates, decay_log = (
        lax.all_to_all(step_size, "inner", split_axis=1, concat_axis=0, tiled=True),
        lax.all_to_all(log_decay, "inner", split_axis=1, concat_axis=0, tiled=True),
    )
    seq_rows = head_inputs.shape[0]
    head_inputs = head_inputs.reshape(seq_rows, heads_dev, head_width)
    scaled = (head_inputs.astype(jnp.float32) * step_rates[:, :, None]).astype(jnp.bfloat16)
    outputs, end_state, block_log, running_all = group_pass(scaled, decay_log, b_rows, c_rows)
    incoming = carry_chain(block_log, end_state)
    carried_term = (
        jnp.einsum("tn,hpn->thp", c_rows.astype(jnp.float32), incoming, precision=MIXED_PREC)
        * jnp.exp(running_all)[:, :, None]
    )
    skip_local = lax.dynamic_slice_in_dim(skip_gain, lax.axis_index("inner") * heads_dev, heads_dev)
    mixed_out = outputs + carried_term + skip_local[None, :, None] * head_inputs.astype(jnp.float32)
    mixed_out = mixed_out.astype(jnp.bfloat16).reshape(seq_rows, heads_dev * head_width)
    return lax.all_to_all(mixed_out, "inner", split_axis=0, concat_axis=1, tiled=True)


def solution(mesh):
    placed = (
        P(("outer", "inner"), None),
        P(("outer", "inner"), None),
        P(("outer", "inner"), None),
        P(("outer", "inner"), None),
        P(("outer", "inner"), None),
        P(),
    )
    return jax.shard_map(
        local, mesh=mesh, in_specs=placed, out_specs=P(("outer", "inner"), None), check_vma=False
    )
```

profile of v0, /device:TPU:0, one launch (start us, length us, event | category | flops | bytes accessed | tf_op | source)
XLA Modules:
  0.0 358.2 jit_solution(7346321738298869880)
XLA Ops:
  0.0 1.6 copy.51
  1.6 6.4 %all-to-all-start.4 = ((f32[256,8,16]{0,2,1:T(8,128)}), f32[256,8,16]{0,2,1:T(8,128)S(1)}, u32[]{:S(2)}, u32[]{:S(2)}) async-start(f32[256,8,16]{0,2,1:T(8,128)} %bitcast.9), calls=%async_computation.4 | async-start | bytes 262144 | tf_op jit(solution)/shard_map/all_to_all | solution.py:108
  8.0 1.2 copy.49
  9.2 1.0 copy.50
  10.2 4.5 %all-to-all-done.4 = f32[256,8,16]{0,2,1:T(8,128)S(1)} async-done(((f32[256,8,16]{0,2,1:T(8,128)}), f32[256,8,16]{0,2,1:T(8,128)S(1)}, u32[]{:S(2)}, u32[]{:S(2)}) %all-to-all-start.4) | async-done | bytes 131104 | tf_op jit(solution)/shard_map/all_to_all | solution.py:108
  14.7 3.5 all-to-all-start.3
  18.2 1.2 copy.47
  19.5 1.0 copy.48
  20.5 13.0 %all-to-all-done.3 = bf16[256,8,128]{2,0,1:T(8,128)(2,1)S(1)} async-done(((bf16[256,8,128]{2,0,1:T(8,128)(2,1)}), bf16[256,8,128]{2,0,1:T(8,128)(2,1)S(1)}, u32[]{:S(2)}, u32[]{:S(2)}) %all-to-all-start.3) | async-done | bytes 524320 | tf_op jit(solution)/shard_map/all_to_all | solution.py:103
  33.5 3.5 all-to-all-start.2
  37.0 6.4 %copy.45 = bf16[256,8192]{0,1:T(8,128)(2,1)} copy(bf16[256,8192]{1,0:T(8,128)(2,1)} %param.6) | data formatting | bytes 8388608 | tf_op args[0]
  43.4 8.9 %all-to-all-done.2 = bf16[256,8,128]{2,0,1:T(8,128)(2,1)S(1)} async-done(((bf16[256,8,128]{2,0,1:T(8,128)(2,1)}), bf16[256,8,128]{2,0,1:T(8,128)(2,1)S(1)}, u32[]{:S(2)}, u32[]{:S(2)}) %all-to-all-start.2) | async-done | bytes 524320 | tf_op jit(solution)/shard_map/all_to_all | solution.py:104
  52.3 4.7 %all-to-all-start = ((bf16[256,8,1024]{0,2,1:T(8,128)(2,1)}), bf16[256,8,1024]{0,2,1:T(8,128)(2,1)}, u32[]{:S(2)}, u32[]{:S(2)}) async-start(bf16[256,8,1024]{0,2,1:T(8,128)(2,1)} %bitcast.156), calls=%async_computation | async-start | bytes 8388608 | tf_op jit(solution)/shard_map/all_to_all | solution.py:102
  57.0 0.7 copy.46
  57.7 0.6 dynamic_slice.14
  58.3 0.6 iota_compare_fusion
  59.0 0.8 broadcast_dynamic-update-slice_fusion
  59.8 4.6 %reduce-window.6 = f32[8,16,2,128]{3,1,2,0:T(8,128)S(1)} reduce-window(f32[8,16,2,128]{3,1,2,0:T(8,128)S(1)} %copy_bitcast_fusion, f32[]{:T(128)} %constant.19.clone.1), window={size=1x1x1x128 pad=0_0x0_0x0_0x127_0}, to_apply=%region_0.1 | reduce-window | flops 4161536 | bytes 262148 | tf_op jit(solution)/shard_map/reduce-window
  64.8 0.2 slice_reduce_fusion
  65.0 0.2 fusion.51
  65.2 0.8 exponential_bitcast_fusion
  66.1 0.8 fusion.36
  66.9 0.5 fusion.50
  67.5 0.4 fusion.29
  67.9 83.0 %all-to-all-done = bf16[256,8,1024]{0,2,1:T(8,128)(2,1)} async-done(((bf16[256,8,1024]{0,2,1:T(8,128)(2,1)}), bf16[256,8,1024]{0,2,1:T(8,128)(2,1)}, u32[]{:S(2)}, u32[]{:S(2)}) %all-to-all-start) | async-done | bytes 4194336 | tf_op jit(solution)/shard_map/all_to_all | solution.py:102
  150.9 3.4 all-to-all-start.1
  154.3 9.6 %convert_bitcast_fusion = (f32[8,256,1024]{1,2,0:T(8,128)}, f32[256,8,1024]{0,2,1:T(8,128)}) fusion(bf16[256,8,1024]{0,2,1:T(8,128)(2,1)} %all-to-all-done), kind=kLoop, calls=%fused_computation.22 | loop fusion | flops 2097152 | bytes 20971520 | tf_op jit(solution)/shard_map/convert_element_type | solution.py:112
  164.0 6.1 %fusion.15 = f32[8,16,64,128]{3,2,1,0:T(8,128)S(1)} fusion(f32[8,256,16]{1,2,0:T(8,128)} %get-tuple-element.56, f32[8,256,16,64]{1,3,2,0:T(8,128)} %bitcast.153, f32[8,256,16]{1,2,0:T(8,128)S(1)} %bitcast.163, bf16[256,8,128]{2,0,1:T(8,128)(2,1)S(1)} %all-to-all-done.3), kind=kOutput, calls=%fused_computation.17 | convolution fusion | flops 1619001344 | bytes 13369344 | tf_op jit(solution)/shard_map/while/body/eval_jaxpr/kshp,ksn->khpn/dot_general | solution.py:38
  170.1 0.4 broadcast_add_fusion
  170.5 3.7 %collective-permute-start = (f32[16,64,128]{2,1,0:T(8,128)S(1)}, f32[16,64,128]{2,1,0:T(8,128)S(1)}, u32[]{:S(2)}, u32[]{:S(2)}) collective-permute-start(f32[16,64,128]{2,1,0:T(8,128)S(1)} %get-tuple-element.45), channel_id=1, source_target_pairs={{0,8},{8,16},{16,24},{1,9},{9,17},{17,25},{2,10},{10,18},{18,26},{... | collective-permute-start | bytes 1572872 | tf_op jit(solution)/shard_map/ppermute | solution.py:14
  174.3 0.2 constant_dynamic-update-slice_fusion.2
  174.7 17.2 %fusion = f32[8,16,64,256]{3,2,1,0:T(8,128)} fusion(f32[8,256,16]{1,2,0:T(8,128)S(1)} %bitcast_bitcast_fusion, f32[8,256,256]{2,1,0:T(8,128)S(1)} %fusion.29, pred[256,256]{1,0:T(8,128)(4,1)S(1)} %copy-done.5, f32[8,256,16,64]{1,3,2,0:T(8,128)S(1)} %bitcast.154, f32[8,256,16]{1,2,0:T(8,128)S(1)} %bitcast.164), kind=kOutput, calls=%fused_computation | convolution fusion | flops 3250585600 | bytes 19202048 | tf_op jit(solution)/shard_map/while/body/eval_jaxpr/ktsh,kshp->kthp/dot_general | solution.py:35
  191.8 0.2 constant_dynamic-update-slice_fusion.1
  192.2 0.3 copy-done.9
  192.6 3.4 collective-permute-start.1
  196.0 0.2 constant_dynamic-update-slice_fusion
  196.3 2.0 copy-done.2
  198.3 9.1 %collective-permute-done.1 = f32[16,64,128]{2,1,0:T(8,128)S(1)} collective-permute-done((f32[16,64,128]{2,1,0:T(8,128)S(1)}, f32[16,64,128]{2,1,0:T(8,128)S(1)}, u32[]{:S(2)}, u32[]{:S(2)}) %collective-permute-start.1) | collective-permute-done | bytes 524320 | tf_op jit(solution)/shard_map/ppermute | solution.py:14
  207.6 4.9 %collective-permute-start.2 = (f32[16,64,128]{2,1,0:T(8,128)S(1)}, f32[16,64,128]{2,1,0:T(8,128)S(1)}, u32[]{:S(2)}, u32[]{:S(2)}) collective-permute-start(f32[16,64,128]{2,1,0:T(8,128)S(1)} %multiply_add_fusion), channel_id=1, source_target_pairs={{0,8},{8,16},{16,24},{1,9},{9,17},{17,25},{2,10},{10,18},{18,26},{... | collective-permute-start | bytes 1572872 | tf_op jit(solution)/shard_map/ppermute | solution.py:14
  212.4 7.8 %fusion.14 = f32[8,16,8,8,256]{4,3,2,1,0:T(8,128)S(1)} fusion(f32[8,16,64,256]{3,2,1,0:T(8,128)} %fusion, f32[8,256,16]{1,2,0:T(8,128)S(1)} %copy-done.3, f32[8,16,64,128]{3,2,1,0:T(8,128)} %copy-done.2, bf16[256,8,128]{2,0,1:T(8,128)(2,1)S(1)} %all-to-all-done.2), kind=kOutput, calls=%fused_computation.16 | convolution fusion | flops 1614807040 | bytes 21626880 | tf_op jit(solution)/shard_map/while/body/eval_jaxpr/ktn,khpn->kthp/dot_general | solution.py:50
  220.3 4.3 %copy.65 = f32[8,16,8,8,256]{4,3,0,2,1:T(8,128)} copy(f32[8,16,8,8,256]{4,3,2,1,0:T(8,128)S(1)} %fusion.14) | data formatting | bytes 16777216 | tf_op jit(solution)/shard_map/reshape | solution.py:71
  224.5 8.1 %copy.58 = f32[8,256,1024]{1,0,2:T(8,128)} copy(f32[8,256,1024]{1,2,0:T(8,128)S(1)} %bitcast.152) | data formatting | bytes 16777216 | tf_op jit(solution)/shard_map/convert_element_type | solution.py:112
  232.6 9.3 %reshape.159 = f32[2048,16,64]{0,2,1:T(8,128)} reshape(f32[8,256,1024]{1,0,2:T(8,128)} %copy.58) | data formatting | bytes 16777216 | tf_op jit(solution)/shard_map/convert_element_type | solution.py:112
  241.9 9.0 %fusion.12 = bf16[2048,16,64]{0,2,1:T(8,128)(2,1)S(1)} fusion(f32[2048,16,64]{0,2,1:T(8,128)} %bitcast.150, f32[2048,16,64]{0,2,1:T(8,128)} %reshape.159, f32[16,64,128]{2,1,0:T(8,128)S(1)} %collective-permute-done.2, bf16[2048,128,1]{1,0,2:T(8,128)(2,1)S(1)} %bitcast.159, f32[16]{0:T(128)S(1)} %copy-done.11, f32[2048,16]{0,1:T(8,128)S(1)} %bitcast.162), kind=kOutput, calls=%fused_computation.13 | convolution fusion | flops 1621098496 | bytes 22151232 | tf_op jit(solution)/shard_map/tn,hpn->thp/dot_general | solution.py:116
  250.9 1.5 copy.67
  252.4 0.9 copy.59
  253.3 98.6 %all_to_all.90 = bf16[8,256,1024]{1,2,0:T(8,128)(2,1)} all-to-all(bf16[8,256,1024]{1,2,0:T(8,128)(2,1)S(1)} %copy.59), channel_id=1, replica_groups=mesh['outer'=4,'inner'=8] {'inner'}, dimensions={0} | all-to-all | bytes 8388608 | tf_op jit(solution)/shard_map/all_to_all | solution.py:122
  351.9 6.3 %copy.60 = bf16[256,8192]{1,0:T(8,128)(2,1)} copy(bf16[256,8192]{0,1:T(8,128)(2,1)} %bitcast.158) | data formatting | bytes 8388608 | tf_op jit(solution)/shard_map/all_to_all | solution.py:122
  (48 shorter events, 1.2 us)
Async XLA Ops:
  1.6 13.1 %all-to-all-start.4 = ((f32[256,8,16]{0,2,1:T(8,128)}), f32[256,8,16]{0,2,1:T(8,128)S(1)}, u32[]{:S(2)}, u32[]{:S(2)}) async-start(f32[256,8,16]{0,2,1:T(8,128)} %bitcast.9), calls=%async_computation.4 | async-start | bytes 262144 | tf_op jit(solution)/shard_map/all_to_all | solution.py:108
  14.7 18.8 %all-to-all-start.3 = ((bf16[256,8,128]{2,0,1:T(8,128)(2,1)}), bf16[256,8,128]{2,0,1:T(8,128)(2,1)S(1)}, u32[]{:S(2)}, u32[]{:S(2)}) async-start(bf16[256,8,128]{2,0,1:T(8,128)(2,1)} %copy.50), calls=%async_computation.3 | async-start | bytes 1048576 | tf_op jit(solution)/shard_map/all_to_all | solution.py:103
  33.5 18.8 %all-to-all-start.2 = ((bf16[256,8,128]{2,0,1:T(8,128)(2,1)}), bf16[256,8,128]{2,0,1:T(8,128)(2,1)S(1)}, u32[]{:S(2)}, u32[]{:S(2)}) async-start(bf16[256,8,128]{2,0,1:T(8,128)(2,1)} %copy.48), calls=%async_computation.2 | async-start | bytes 1048576 | tf_op jit(solution)/shard_map/all_to_all | solution.py:104
  52.3 4.7 %copy-start.4 = (f32[256,128]{1,0:T(8,128)S(1)}, f32[256,128]{1,0:T(8,128)}, u32[]{:S(2)}) copy-start(f32[256,128]{1,0:T(8,128)} %param.7) | copy-start | bytes 393220
  52.3 5.5 %copy-start.13 = (f32[128]{0:T(128)S(1)}, f32[128]{0:T(128)}, u32[]{:S(2)}) copy-start(f32[128]{0:T(128)} %param.11) | copy-start | bytes 1540
  52.3 98.7 %all-to-all-start = ((bf16[256,8,1024]{0,2,1:T(8,128)(2,1)}), bf16[256,8,1024]{0,2,1:T(8,128)(2,1)}, u32[]{:S(2)}, u32[]{:S(2)}) async-start(bf16[256,8,1024]{0,2,1:T(8,128)(2,1)} %bitcast.156), calls=%async_computation | async-start | bytes 8388608 | tf_op jit(solution)/shard_map/all_to_all | solution.py:102
  150.9 13.0 %all-to-all-start.1 = ((f32[256,8,16]{0,2,1:T(8,128)}), f32[256,8,16]{0,2,1:T(8,128)S(1)}, u32[]{:S(2)}, u32[]{:S(2)}) async-start(f32[256,8,16]{0,2,1:T(8,128)} %bitcast.165), calls=%async_computation.1 | async-start | bytes 262144 | tf_op jit(solution)/shard_map/all_to_all | solution.py:107
  163.9 6.2 %copy-start.6 = (f32[16]{0:T(128)S(1)}, f32[16]{0:T(128)}, u32[]{:S(2)}) copy-start(f32[16]{0:T(128)} %get-tuple-element.27) | copy-start | bytes 196
  163.9 6.2 %copy-start.7 = (f32[16]{0:T(128)S(1)}, f32[16]{0:T(128)}, u32[]{:S(2)}) copy-start(f32[16]{0:T(128)} %get-tuple-element.29) | copy-start | bytes 196
  163.9 6.2 %copy-start.8 = (f32[16]{0:T(128)S(1)}, f32[16]{0:T(128)}, u32[]{:S(2)}) copy-start(f32[16]{0:T(128)} %get-tuple-element.42) | copy-start | bytes 196
  163.9 6.2 %copy-start.10 = (f32[16]{0:T(128)S(1)}, f32[16]{0:T(128)}, u32[]{:S(2)}) copy-start(f32[16]{0:T(128)} %get-tuple-element.25) | copy-start | bytes 196
  163.9 6.2 %copy-start.12 = (f32[16]{0:T(128)S(1)}, f32[16]{0:T(128)}, u32[]{:S(2)}) copy-start(f32[16]{0:T(128)} %get-tuple-element.59) | copy-start | bytes 196
  163.9 10.3 %copy-start.1 = (f32[8,16,64,128]{3,2,1,0:T(8,128)S(1)}, f32[8,16,64,128]{3,2,1,0:T(8,128)}, u32[]{:S(2)}) copy-start(f32[8,16,64,128]{3,2,1,0:T(8,128)} %broadcast_dynamic-update-slice_fusion) | copy-start | bytes 12582916
  170.1 4.6 %copy-start = (f32[256,8,1024]{0,2,1:T(8,128)S(1)}, f32[256,8,1024]{0,2,1:T(8,128)}, u32[]{:S(2)}) copy-start(f32[256,8,1024]{0,2,1:T(8,128)} %get-tuple-element.54) | copy-start | bytes 25165828
  170.1 4.6 %copy-start.5 = (pred[256,256]{1,0:T(8,128)(4,1)S(1)}, pred[256,256]{1,0:T(8,128)(4,1)}, u32[]{:S(2)}) copy-start(pred[256,256]{1,0:T(8,128)(4,1)} %iota_compare_fusion) | copy-start | bytes 196612
  170.5 21.7 %collective-permute-start = (f32[16,64,128]{2,1,0:T(8,128)S(1)}, f32[16,64,128]{2,1,0:T(8,128)S(1)}, u32[]{:S(2)}, u32[]{:S(2)}) collective-permute-start(f32[16,64,128]{2,1,0:T(8,128)S(1)} %get-tuple-element.45), channel_id=1, source_target_pairs={{0,8},{8,16},{16,24},{1,9},{9,17},{17,25},{2,10},{10,18},{18,26},{... | collective-permute-start | bytes 1572872 | tf_op jit(solution)/shard_map/ppermute | solution.py:14
  191.8 0.6 copy-start.9
  192.1 20.4 %copy-start.3 = (f32[8,256,16]{1,2,0:T(8,128)S(1)}, f32[8,256,16]{1,2,0:T(8,128)}, u32[]{:S(2)}) copy-start(f32[8,256,16]{1,2,0:T(8,128)} %get-tuple-element.57) | copy-start | bytes 393220
  192.6 14.8 %collective-permute-start.1 = (f32[16,64,128]{2,1,0:T(8,128)S(1)}, f32[16,64,128]{2,1,0:T(8,128)S(1)}, u32[]{:S(2)}, u32[]{:S(2)}) collective-permute-start(f32[16,64,128]{2,1,0:T(8,128)S(1)} %multiply_add_fusion.1), channel_id=1, source_target_pairs={{0,8},{8,16},{16,24},{1,9},{9,17},{17,25},{2,10},{10,18},{18,26},{... | collective-permute-start | bytes 1572872 | tf_op jit(solution)/shard_map/ppermute | solution.py:14
  196.3 2.0 copy-start.2
  207.4 17.1 %slice-start = ((s8[8388608]{0:T(1024)(128)(4,1)}), s8[4194304]{0:T(1024)(128)(4,1)S(1)}, s32[]{:S(2)}) async-start(s8[8388608]{0:T(1024)(128)(4,1)} %bitcast.151), calls=%async_computation.6 | async-start | bytes 8388608
  207.6 34.3 %collective-permute-start.2 = (f32[16,64,128]{2,1,0:T(8,128)S(1)}, f32[16,64,128]{2,1,0:T(8,128)S(1)}, u32[]{:S(2)}, u32[]{:S(2)}) collective-permute-start(f32[16,64,128]{2,1,0:T(8,128)S(1)} %multiply_add_fusion), channel_id=1, source_target_pairs={{0,8},{8,16},{16,24},{1,9},{9,17},{17,25},{2,10},{10,18},{18,26},{... | collective-permute-start | bytes 1572872 | tf_op jit(solution)/shard_map/ppermute | solution.py:14
  212.4 12.1 %slice-start.1 = ((s8[8388608]{0:T(1024)(128)(4,1)}), s8[4194304]{0:T(1024)(128)(4,1)S(1)}, s32[]{:S(2)}) async-start(s8[8388608]{0:T(1024)(128)(4,1)} %bitcast.151), calls=%async_computation.7 | async-start | bytes 8388608
  232.6 9.3 %copy-start.11 = (f32[16]{0:T(128)S(1)}, f32[16]{0:T(128)}, u32[]{:S(2)}) copy-start(f32[16]{0:T(128)} %dynamic_slice.14) | copy-start | bytes 196
where the time goes:
time: 359 us; the launch traced here: 358 us
  waiting for transfers between devices  119 us (33%)
  blocking collectives  98.6 us (27%)
  local copies, waits for them, and re-layouts  47.6 us (13%)
  matrix products  40.5 us (11%)
  starting transfers between devices  33.4 us (9%)
  other arithmetic  19.2 us (5%)
    all_to_all x1, blocking collectives, local(): lax.all_to_all(mixed_out, 'inner', split_axis=0, concat_axis=1, tiled=True)  98.6 us
    all_to_all x1, waiting for transfers between devices, local(): lax.all_to_all(inputs, 'inner', split_axis=1, concat_axis=0, tiled=True)  83 us
    convert_element_type x2, local copies, waits for them, and re-layouts, local(): head_inputs.astype(jnp.float32) * step_rates[:, :, None]  17.4 us
    dot_general x1, matrix products, advance(): jnp.einsum('ktsh,kshp->kthp', weights, as_float, precision=MIXED_PREC)  17.2 us
    unnamed x39, local copies, waits for them, and re-layouts  15.9 us
    all_to_all x1, waiting for transfers between devices, local(): lax.all_to_all(b_copy, 'inner', split_axis=1, concat_axis=0, tiled=True)  13 us
    ppermute x3, starting transfers between devices, passed_along(): return lax.ppermute(block, axis, route)  12 us
    convert_element_type x1, other arithmetic, local(): head_inputs.astype(jnp.float32) * step_rates[:, :, None]  9.6 us
  transfers between devices with their start and end apart: 8, of which 5 were waited for; matrix products, arithmetic and copies ran while one was open for 22% of the time, Pallas kernels for 0%

commit v1 on v0

--- a/solution.py
+++ b/solution.py
@@ -119,7 +119,12 @@
     skip_local = lax.dynamic_slice_in_dim(skip_gain, lax.axis_index("inner") * heads_dev, heads_dev)
     mixed_out = outputs + carried_term + skip_local[None, :, None] * head_inputs.astype(jnp.float32)
     mixed_out = mixed_out.astype(jnp.bfloat16).reshape(seq_rows, heads_dev * head_width)
-    return lax.all_to_all(mixed_out, "inner", split_axis=0, concat_axis=1, tiled=True)
+    return jnp.concatenate(
+        lax.all_to_all(
+            jnp.stack(jnp.split(mixed_out, lax.axis_size("inner"), axis=0)), "inner", 0, 0
+        ),
+        axis=1,
+    )
 
 
 def solution(mesh):

time: 359 us -> 358 us (level)
    all_to_all x2 -> x0, local copies, waits for them, and re-layouts: 7.18 us -> none  [local(): lax.all_to_all(mixed_out, 'inner', split_axis=0, concat_axis=1, tiled=True)]
    reshape x1 -> x2, local copies, waits for them, and re-layouts: 0.01 us -> 6.32 us  [the longest x1 6.32 us: local(): jnp.concatenate(lax.all_to_all(jnp.stack(jnp.split(mixed_out, lax.axis_si...]
    unnamed x39 -> x45, local copies, waits for them, and re-layouts: 15.9 us -> 14.7 us
where the time goes in v1:
time: 358 us; the launch traced here: 357 us
  waiting for transfers between devices  119 us (33%)
  blocking collectives  98.6 us (28%)
  local copies, waits for them, and re-layouts  46.1 us (13%)
  matrix products  40.5 us (11%)
  starting transfers between devices  33.4 us (9%)
  other arithmetic  19.2 us (5%)
    all_to_all x1, blocking collectives, local(): lax.all_to_all(jnp.stack(jnp.split(mixed_out, lax.axis_size('inner'), axi...  98.6 us
    all_to_all x1, waiting for transfers between devices, local(): lax.all_to_all(inputs, 'inner', split_axis=1, concat_axis=0, tiled=True)  83 us
    convert_element_type x2, local copies, waits for them, and re-layouts, local(): head_inputs.astype(jnp.float32) * step_rates[:, :, None]  17.4 us
    dot_general x1, matrix products, advance(): jnp.einsum('ktsh,kshp->kthp', weights, as_float, precision=MIXED_PREC)  17.2 us
    unnamed x45, local copies, waits for them, and re-layouts  14.7 us
    all_to_all x1, waiting for transfers between devices, local(): lax.all_to_all(b_copy, 'inner', split_axis=1, concat_axis=0, tiled=True)  13 us
    ppermute x3, starting transfers between devices, passed_along(): return lax.ppermute(block, axis, route)  12 us
    convert_element_type x1, other arithmetic, local(): head_inputs.astype(jnp.float32) * step_rates[:, :, None]  9.6 us
  transfers between devices with their start and end apart: 8, of which 5 were waited for; matrix products, arithmetic and copies ran while one was open for 22% of the time, Pallas kernels for 0%

profile of v1, /device:TPU:0, one launch (start us, length us, event | category | flops | bytes accessed | tf_op | source)
XLA Modules:
  0.0 356.8 jit_solution(176809697345480502)
XLA Ops:
  0.0 1.6 copy.51
  1.6 6.4 %all-to-all-start.4 = ((f32[256,8,16]{0,2,1:T(8,128)}), f32[256,8,16]{0,2,1:T(8,128)S(1)}, u32[]{:S(2)}, u32[]{:S(2)}) async-start(f32[256,8,16]{0,2,1:T(8,128)} %bitcast.9), calls=%async_computation.4 | async-start | bytes 262144 | tf_op jit(solution)/shard_map/all_to_all | solution.py:108
  8.0 1.2 copy.49
  9.2 1.0 copy.50
  10.2 4.5 %all-to-all-done.4 = f32[256,8,16]{0,2,1:T(8,128)S(1)} async-done(((f32[256,8,16]{0,2,1:T(8,128)}), f32[256,8,16]{0,2,1:T(8,128)S(1)}, u32[]{:S(2)}, u32[]{:S(2)}) %all-to-all-start.4) | async-done | bytes 131104 | tf_op jit(solution)/shard_map/all_to_all | solution.py:108
  14.7 3.5 all-to-all-start.3
  18.2 1.2 copy.47
  19.5 1.0 copy.48
  20.5 13.0 %all-to-all-done.3 = bf16[256,8,128]{2,0,1:T(8,128)(2,1)S(1)} async-done(((bf16[256,8,128]{2,0,1:T(8,128)(2,1)}), bf16[256,8,128]{2,0,1:T(8,128)(2,1)S(1)}, u32[]{:S(2)}, u32[]{:S(2)}) %all-to-all-start.3) | async-done | bytes 524320 | tf_op jit(solution)/shard_map/all_to_all | solution.py:103
  33.5 3.5 all-to-all-start.2
  37.0 6.4 %copy.45 = bf16[256,8192]{0,1:T(8,128)(2,1)} copy(bf16[256,8192]{1,0:T(8,128)(2,1)} %param.6) | data formatting | bytes 8388608 | tf_op args[0]
  43.4 8.9 %all-to-all-done.2 = bf16[256,8,128]{2,0,1:T(8,128)(2,1)S(1)} async-done(((bf16[256,8,128]{2,0,1:T(8,128)(2,1)}), bf16[256,8,128]{2,0,1:T(8,128)(2,1)S(1)}, u32[]{:S(2)}, u32[]{:S(2)}) %all-to-all-start.2) | async-done | bytes 524320 | tf_op jit(solution)/shard_map/all_to_all | solution.py:104
  52.3 4.7 %all-to-all-start = ((bf16[256,8,1024]{0,2,1:T(8,128)(2,1)}), bf16[256,8,1024]{0,2,1:T(8,128)(2,1)}, u32[]{:S(2)}, u32[]{:S(2)}) async-start(bf16[256,8,1024]{0,2,1:T(8,128)(2,1)} %bitcast.158), calls=%async_computation | async-start | bytes 8388608 | tf_op jit(solution)/shard_map/all_to_all | solution.py:102
  57.0 0.7 copy.46
  57.7 0.6 dynamic_slice.14
  58.3 0.6 iota_compare_fusion
  59.0 0.8 broadcast_dynamic-update-slice_fusion
  59.8 4.6 %reduce-window.6 = f32[8,16,2,128]{3,1,2,0:T(8,128)S(1)} reduce-window(f32[8,16,2,128]{3,1,2,0:T(8,128)S(1)} %copy_bitcast_fusion, f32[]{:T(128)} %constant.19.clone.1), window={size=1x1x1x128 pad=0_0x0_0x0_0x127_0}, to_apply=%region_0.1 | reduce-window | flops 4161536 | bytes 262148 | tf_op jit(solution)/shard_map/reduce-window
  64.5 0.2 copy.53
  64.8 0.2 slice_reduce_fusion
  65.0 0.2 fusion.52
  65.2 0.8 exponential_bitcast_fusion
  66.1 0.8 fusion.36
  66.9 0.5 fusion.51
  67.5 0.4 fusion.29
  67.9 83.0 %all-to-all-done = bf16[256,8,1024]{0,2,1:T(8,128)(2,1)} async-done(((bf16[256,8,1024]{0,2,1:T(8,128)(2,1)}), bf16[256,8,1024]{0,2,1:T(8,128)(2,1)}, u32[]{:S(2)}, u32[]{:S(2)}) %all-to-all-start) | async-done | bytes 4194336 | tf_op jit(solution)/shard_map/all_to_all | solution.py:102
  150.9 3.4 all-to-all-start.1
  154.3 9.6 %convert_bitcast_fusion = (f32[8,256,1024]{1,2,0:T(8,128)}, f32[256,8,1024]{0,2,1:T(8,128)}) fusion(bf16[256,8,1024]{0,2,1:T(8,128)(2,1)} %all-to-all-done), kind=kLoop, calls=%fused_computation.22 | loop fusion | flops 2097152 | bytes 20971520 | tf_op jit(solution)/shard_map/convert_element_type | solution.py:112
  164.0 6.1 %fusion.15 = f32[8,16,64,128]{3,2,1,0:T(8,128)S(1)} fusion(f32[8,256,16]{1,2,0:T(8,128)} %get-tuple-element.64, f32[8,256,16,64]{1,3,2,0:T(8,128)} %bitcast.156, f32[8,256,16]{1,2,0:T(8,128)S(1)} %bitcast.172, bf16[256,8,128]{2,0,1:T(8,128)(2,1)S(1)} %all-to-all-done.3), kind=kOutput, calls=%fused_computation.17 | convolution fusion | flops 1619001344 | bytes 13369344 | tf_op jit(solution)/shard_map/while/body/eval_jaxpr/kshp,ksn->khpn/dot_general | solution.py:38
  170.1 0.4 broadcast_add_fusion
  170.5 3.7 %collective-permute-start = (f32[16,64,128]{2,1,0:T(8,128)S(1)}, f32[16,64,128]{2,1,0:T(8,128)S(1)}, u32[]{:S(2)}, u32[]{:S(2)}) collective-permute-start(f32[16,64,128]{2,1,0:T(8,128)S(1)} %get-tuple-element.45), channel_id=1, source_target_pairs={{0,8},{8,16},{16,24},{1,9},{9,17},{17,25},{2,10},{10,18},{18,26},{... | collective-permute-start | bytes 1572872 | tf_op jit(solution)/shard_map/ppermute | solution.py:14
  174.3 0.2 constant_dynamic-update-slice_fusion.2
  174.7 17.2 %fusion = f32[8,16,64,256]{3,2,1,0:T(8,128)} fusion(f32[8,256,16]{1,2,0:T(8,128)S(1)} %bitcast_bitcast_fusion, f32[8,256,256]{2,1,0:T(8,128)S(1)} %fusion.29, pred[256,256]{1,0:T(8,128)(4,1)S(1)} %copy-done.5, f32[8,256,16,64]{1,3,2,0:T(8,128)S(1)} %bitcast.157, f32[8,256,16]{1,2,0:T(8,128)S(1)} %bitcast.173), kind=kOutput, calls=%fused_computation | convolution fusion | flops 3250585600 | bytes 19202048 | tf_op jit(solution)/shard_map/while/body/eval_jaxpr/ktsh,kshp->kthp/dot_general | solution.py:35
  191.8 0.2 constant_dynamic-update-slice_fusion.1
  192.2 0.3 copy-done.9
  192.6 3.4 collective-permute-start.1
  196.0 0.2 constant_dynamic-update-slice_fusion
  196.3 2.0 copy-done.2
  198.3 9.1 %collective-permute-done.1 = f32[16,64,128]{2,1,0:T(8,128)S(1)} collective-permute-done((f32[16,64,128]{2,1,0:T(8,128)S(1)}, f32[16,64,128]{2,1,0:T(8,128)S(1)}, u32[]{:S(2)}, u32[]{:S(2)}) %collective-permute-start.1) | collective-permute-done | bytes 524320 | tf_op jit(solution)/shard_map/ppermute | solution.py:14
  207.6 4.9 %collective-permute-start.2 = (f32[16,64,128]{2,1,0:T(8,128)S(1)}, f32[16,64,128]{2,1,0:T(8,128)S(1)}, u32[]{:S(2)}, u32[]{:S(2)}) collective-permute-start(f32[16,64,128]{2,1,0:T(8,128)S(1)} %multiply_add_fusion), channel_id=1, source_target_pairs={{0,8},{8,16},{16,24},{1,9},{9,17},{17,25},{2,10},{10,18},{18,26},{... | collective-permute-start | bytes 1572872 | tf_op jit(solution)/shard_map/ppermute | solution.py:14
  212.4 7.8 %fusion.14 = f32[8,16,8,8,256]{4,3,2,1,0:T(8,128)S(1)} fusion(f32[8,16,64,256]{3,2,1,0:T(8,128)} %fusion, f32[8,256,16]{1,2,0:T(8,128)S(1)} %copy-done.3, f32[8,16,64,128]{3,2,1,0:T(8,128)} %copy-done.2, bf16[256,8,128]{2,0,1:T(8,128)(2,1)S(1)} %all-to-all-done.2), kind=kOutput, calls=%fused_computation.16 | convolution fusion | flops 1614807040 | bytes 21626880 | tf_op jit(solution)/shard_map/while/body/eval_jaxpr/ktn,khpn->kthp/dot_general | solution.py:50
  220.3 4.3 %copy.65 = f32[8,16,8,8,256]{4,3,0,2,1:T(8,128)} copy(f32[8,16,8,8,256]{4,3,2,1,0:T(8,128)S(1)} %fusion.14) | data formatting | bytes 16777216 | tf_op jit(solution)/shard_map/reshape | solution.py:71
  224.5 8.1 %copy.58 = f32[8,256,1024]{1,0,2:T(8,128)} copy(f32[8,256,1024]{1,2,0:T(8,128)S(1)} %bitcast.155) | data formatting | bytes 16777216 | tf_op jit(solution)/shard_map/convert_element_type | solution.py:112
  232.6 9.3 %reshape.179 = f32[2048,16,64]{0,2,1:T(8,128)} reshape(f32[8,256,1024]{1,0,2:T(8,128)} %copy.58) | data formatting | bytes 16777216 | tf_op jit(solution)/shard_map/convert_element_type | solution.py:112
  241.9 9.0 %fusion.12 = bf16[2048,16,64]{0,2,1:T(8,128)(2,1)S(1)} fusion(f32[2048,16,64]{0,2,1:T(8,128)} %bitcast.153, f32[2048,16,64]{0,2,1:T(8,128)} %reshape.179, f32[16,64,128]{2,1,0:T(8,128)S(1)} %collective-permute-done.2, bf16[2048,128,1]{1,0,2:T(8,128)(2,1)S(1)} %bitcast.160, f32[16]{0:T(128)S(1)} %copy-done.11, f32[2048,16]{0,1:T(8,128)S(1)} %bitcast.171), kind=kOutput, calls=%fused_computation.13 | convolution fusion | flops 1621098496 | bytes 22151232 | tf_op jit(solution)/shard_map/tn,hpn->thp/dot_general | solution.py:116
  250.9 0.6 fusion.50
  251.8 98.6 %all_to_all.76 = bf16[8,256,1024]{1,2,0:T(8,128)(2,1)} all-to-all(bf16[8,256,1024]{1,2,0:T(8,128)(2,1)S(1)} %constant_dynamic-update-slice_fusion.3), channel_id=1, replica_groups=mesh['outer'=4,'inner'=8] {'inner'}, dimensions={0} | all-to-all | bytes 8388608 | tf_op jit(solution)/shard_map/all_to_all | solution.py:123
  350.5 6.3 %copy.62 = bf16[256,8192]{1,0:T(8,128)(2,1)} copy(bf16[256,8192]{0,1:T(8,128)(2,1)} %bitcast.159) | data formatting | bytes 8388608 | tf_op jit(solution)/shard_map/reshape | solution.py:122
  (55 shorter events, 1.4 us)
Async XLA Ops:
  1.6 13.1 %all-to-all-start.4 = ((f32[256,8,16]{0,2,1:T(8,128)}), f32[256,8,16]{0,2,1:T(8,128)S(1)}, u32[]{:S(2)}, u32[]{:S(2)}) async-start(f32[256,8,16]{0,2,1:T(8,128)} %bitcast.9), calls=%async_computation.4 | async-start | bytes 262144 | tf_op jit(solution)/shard_map/all_to_all | solution.py:108
  14.7 18.8 %all-to-all-start.3 = ((bf16[256,8,128]{2,0,1:T(8,128)(2,1)}), bf16[256,8,128]{2,0,1:T(8,128)(2,1)S(1)}, u32[]{:S(2)}, u32[]{:S(2)}) async-start(bf16[256,8,128]{2,0,1:T(8,128)(2,1)} %copy.50), calls=%async_computation.3 | async-start | bytes 1048576 | tf_op jit(solution)/shard_map/all_to_all | solution.py:103
  33.5 18.8 %all-to-all-start.2 = ((bf16[256,8,128]{2,0,1:T(8,128)(2,1)}), bf16[256,8,128]{2,0,1:T(8,128)(2,1)S(1)}, u32[]{:S(2)}, u32[]{:S(2)}) async-start(bf16[256,8,128]{2,0,1:T(8,128)(2,1)} %copy.48), calls=%async_computation.2 | async-start | bytes 1048576 | tf_op jit(solution)/shard_map/all_to_all | solution.py:104
  52.3 4.7 %copy-start.4 = (f32[256,128]{1,0:T(8,128)S(1)}, f32[256,128]{1,0:T(8,128)}, u32[]{:S(2)}) copy-start(f32[256,128]{1,0:T(8,128)} %param.7) | copy-start | bytes 393220
  52.3 5.5 %copy-start.13 = (f32[128]{0:T(128)S(1)}, f32[128]{0:T(128)}, u32[]{:S(2)}) copy-start(f32[128]{0:T(128)} %param.11) | copy-start | bytes 1540
  52.3 98.7 %all-to-all-start = ((bf16[256,8,1024]{0,2,1:T(8,128)(2,1)}), bf16[256,8,1024]{0,2,1:T(8,128)(2,1)}, u32[]{:S(2)}, u32[]{:S(2)}) async-start(bf16[256,8,1024]{0,2,1:T(8,128)(2,1)} %bitcast.158), calls=%async_computation | async-start | bytes 8388608 | tf_op jit(solution)/shard_map/all_to_all | solution.py:102
  150.9 13.0 %all-to-all-start.1 = ((f32[256,8,16]{0,2,1:T(8,128)}), f32[256,8,16]{0,2,1:T(8,128)S(1)}, u32[]{:S(2)}, u32[]{:S(2)}) async-start(f32[256,8,16]{0,2,1:T(8,128)} %bitcast.174), calls=%async_computation.1 | async-start | bytes 262144 | tf_op jit(solution)/shard_map/all_to_all | solution.py:107
  163.9 6.2 %copy-start.6 = (f32[16]{0:T(128)S(1)}, f32[16]{0:T(128)}, u32[]{:S(2)}) copy-start(f32[16]{0:T(128)} %get-tuple-element.27) | copy-start | bytes 196
  163.9 6.2 %copy-start.7 = (f32[16]{0:T(128)S(1)}, f32[16]{0:T(128)}, u32[]{:S(2)}) copy-start(f32[16]{0:T(128)} %get-tuple-element.29) | copy-start | bytes 196
  163.9 6.2 %copy-start.8 = (f32[16]{0:T(128)S(1)}, f32[16]{0:T(128)}, u32[]{:S(2)}) copy-start(f32[16]{0:T(128)} %get-tuple-element.42) | copy-start | bytes 196
  163.9 6.2 %copy-start.10 = (f32[16]{0:T(128)S(1)}, f32[16]{0:T(128)}, u32[]{:S(2)}) copy-start(f32[16]{0:T(128)} %get-tuple-element.25) | copy-start | bytes 196
  163.9 6.2 %copy-start.12 = (f32[16]{0:T(128)S(1)}, f32[16]{0:T(128)}, u32[]{:S(2)}) copy-start(f32[16]{0:T(128)} %get-tuple-element.67) | copy-start | bytes 196
  163.9 10.3 %copy-start.1 = (f32[8,16,64,128]{3,2,1,0:T(8,128)S(1)}, f32[8,16,64,128]{3,2,1,0:T(8,128)}, u32[]{:S(2)}) copy-start(f32[8,16,64,128]{3,2,1,0:T(8,128)} %broadcast_dynamic-update-slice_fusion) | copy-start | bytes 12582916
  170.1 4.6 %copy-start = (f32[256,8,1024]{0,2,1:T(8,128)S(1)}, f32[256,8,1024]{0,2,1:T(8,128)}, u32[]{:S(2)}) copy-start(f32[256,8,1024]{0,2,1:T(8,128)} %get-tuple-element.62) | copy-start | bytes 25165828
  170.1 4.6 %copy-start.5 = (pred[256,256]{1,0:T(8,128)(4,1)S(1)}, pred[256,256]{1,0:T(8,128)(4,1)}, u32[]{:S(2)}) copy-start(pred[256,256]{1,0:T(8,128)(4,1)} %iota_compare_fusion) | copy-start | bytes 196612
  170.5 21.7 %collective-permute-start = (f32[16,64,128]{2,1,0:T(8,128)S(1)}, f32[16,64,128]{2,1,0:T(8,128)S(1)}, u32[]{:S(2)}, u32[]{:S(2)}) collective-permute-start(f32[16,64,128]{2,1,0:T(8,128)S(1)} %get-tuple-element.45), channel_id=1, source_target_pairs={{0,8},{8,16},{16,24},{1,9},{9,17},{17,25},{2,10},{10,18},{18,26},{... | collective-permute-start | bytes 1572872 | tf_op jit(solution)/shard_map/ppermute | solution.py:14
  191.8 0.6 copy-start.9
  192.1 20.4 %copy-start.3 = (f32[8,256,16]{1,2,0:T(8,128)S(1)}, f32[8,256,16]{1,2,0:T(8,128)}, u32[]{:S(2)}) copy-start(f32[8,256,16]{1,2,0:T(8,128)} %get-tuple-element.65) | copy-start | bytes 393220
  192.6 14.8 %collective-permute-start.1 = (f32[16,64,128]{2,1,0:T(8,128)S(1)}, f32[16,64,128]{2,1,0:T(8,128)S(1)}, u32[]{:S(2)}, u32[]{:S(2)}) collective-permute-start(f32[16,64,128]{2,1,0:T(8,128)S(1)} %multiply_add_fusion.1), channel_id=1, source_target_pairs={{0,8},{8,16},{16,24},{1,9},{9,17},{17,25},{2,10},{10,18},{18,26},{... | collective-permute-start | bytes 1572872 | tf_op jit(solution)/shard_map/ppermute | solution.py:14
  196.3 2.0 copy-start.2
  207.4 17.1 %slice-start = ((s8[8388608]{0:T(1024)(128)(4,1)}), s8[4194304]{0:T(1024)(128)(4,1)S(1)}, s32[]{:S(2)}) async-start(s8[8388608]{0:T(1024)(128)(4,1)} %bitcast.154), calls=%async_computation.6 | async-start | bytes 8388608
  207.6 34.3 %collective-permute-start.2 = (f32[16,64,128]{2,1,0:T(8,128)S(1)}, f32[16,64,128]{2,1,0:T(8,128)S(1)}, u32[]{:S(2)}, u32[]{:S(2)}) collective-permute-start(f32[16,64,128]{2,1,0:T(8,128)S(1)} %multiply_add_fusion), channel_id=1, source_target_pairs={{0,8},{8,16},{16,24},{1,9},{9,17},{17,25},{2,10},{10,18},{18,26},{... | collective-permute-start | bytes 1572872 | tf_op jit(solution)/shard_map/ppermute | solution.py:14
  212.4 12.1 %slice-start.1 = ((s8[8388608]{0:T(1024)(128)(4,1)}), s8[4194304]{0:T(1024)(128)(4,1)S(1)}, s32[]{:S(2)}) async-start(s8[8388608]{0:T(1024)(128)(4,1)} %bitcast.154), calls=%async_computation.7 | async-start | bytes 8388608
  232.6 9.3 %copy-start.11 = (f32[16]{0:T(128)S(1)}, f32[16]{0:T(128)}, u32[]{:S(2)}) copy-start(f32[16]{0:T(128)} %dynamic_slice.14) | copy-start | bytes 196
